TPU v7x, 32 devices: a whole 2x2x4 slice. The times are simulated.
32 devices in a mesh: copy: 2 (over y), grid: 4 (over z), blk: 2 (over x), sub: 2 (over core).
Axes of the slice: x: 2, y: 2, z: 4, core: 2. Of those that a mesh axis runs over, the one named last changes fastest.
Arguments:
- ensemble: float32 [128, 3, 256, 1024], P(('copy', 'grid'), None, 'blk', 'sub'), parts along dimension 0, may hold values from -6 to 6
- basin_thickness: float32 [512, 1024], P(('copy', 'blk'), 'sub'), parts along dimension 0, may hold values from 0.25 to 2
- wet_indicator: int32 [512, 1024], P(('copy', 'blk'), 'sub'), parts along dimension 0, may hold values 0 or 1
- obs_cell: int32 [4, 4, 2, 64], P(('copy', 'blk'), 'grid', 'sub'), parts along dimension 0, may hold values from 0 to 16383
- obs_count: int32 [4, 4, 2], P(('copy', 'blk'), 'grid', 'sub'), parts along dimension 0, may hold values from 16 to 64, as said below
- obs_value: float32 [4, 4, 2, 64], P(('copy', 'blk'), 'grid', 'sub'), parts along dimension 0, may hold values from -6 to 6
- obs_error: float32 [4, 4, 2, 64], P(('copy', 'blk'), 'grid', 'sub'), parts along dimension 0, may hold values from 0.5 to 2
Outputs:
- analysis: float32 [128, 3, 2, 128, 1024], P('copy', None, 'blk', 'grid', 'sub'), parts along dimension 0
There are 2 independent parts, one for each index of `copy`. A program takes and returns all parts, laid end to end along the dimension named above; each array names one. Nothing has to cross between parts.
Inputs may be any that keep to these rules, and one draw needn't show every extreme that they name: `obs_count`: one block of every draw has all 64 slots live.
All inputs are finite; a program needn't handle non-finite values. No bound on the sum of `wet_indicator` on one device may be relied on, other than what follows from the above.
Results may differ from a plain program's by a relative error of at most 0.0003.
Values sent between devices are 32-bit elements; how exact they have to be, the bound alone decides.
No kernel may reach another device: no remote copies, remote signals or barrier semaphores. Data moves between devices by JAX's collectives and lax.ppermute only.
A program may use at most 128 MiB of HBM per device.

v0:
```python
import math
import jax
import jax.numpy as jnp
from jax import lax
from jax.sharding import PartitionSpec as P

STEPS = 2
NS_STEPS = 8
FRICTION = 0.05
PRESSURE = 0.35
DIVERGE = 0.35
CORIOLIS = 0.2
precise = lax.Precision.HIGHEST


def padded(cells, sides, width):
    for axis, dim in sides:
        count = lax.axis_size(axis)
        ends = count - 1
        head = lax.slice_in_dim(cells, 0, width, axis=dim)
        tail = lax.slice_in_dim(cells, cells.shape[dim] - width, cells.shape[dim], axis=dim)
        cells = jnp.concatenate(
            [
                lax.ppermute(tail, axis, [(i, (i + 1) % count) for i in range(ends)]),
                cells,
                lax.ppermute(head, axis, [((i + 1) % count, i) for i in range(ends)]),
            ],
            axis=dim,
        )
    return cells


def thin_step(dynamic_vector, static_local, inner_cor):
    height = dynamic_vector[:, 0]
    bordered_array = padded(height, (("blk", 1), ("sub", 2)), 1)
    inner_depth = static_local[0]
    interior_indicator = static_local[1]
    grad_first = bordered_array[:, 2:, 1:-1] - bordered_array[:, :-2, 1:-1]
    grad_second = bordered_array[:, 1:-1, 2:] - bordered_array[:, 1:-1, :-2]
    first_new = interior_indicator * (
        (1.0 - FRICTION) * dynamic_vector[:, 1]
        + inner_cor * dynamic_vector[:, 2]
        - PRESSURE * grad_first
    )
    second_new = interior_indicator * (
        (1.0 - FRICTION) * dynamic_vector[:, 2]
        - inner_cor * dynamic_vector[:, 1]
        - PRESSURE * grad_second
    )
    fluxes = jnp.stack([inner_depth * first_new, inner_depth * second_new], axis=1)
    flux_wide = padded(fluxes, (("blk", 2), ("sub", 3)), 1)
    divergence = (
        flux_wide[:, 0, 2:, 1:-1]
        - flux_wide[:, 0, :-2, 1:-1]
        + (flux_wide[:, 1, 1:-1, 2:] - flux_wide[:, 1, 1:-1, :-2])
    )
    height_new = height - DIVERGE * divergence
    return jnp.stack([height_new, first_new, second_new], axis=1)


def observe(surface_height, obs_cell, obs_count, obs_value, obs_error):
    members = surface_height.shape[0]
    flat = surface_height.reshape(members, -1)
    cells = obs_cell.reshape(-1)
    picked = jnp.take(flat, cells, axis=1)
    pbar = jnp.mean(picked, axis=0)
    valid = jnp.arange(cells.shape[0], dtype=jnp.int32) < obs_count.reshape(())
    scale = jnp.where(valid, 1.0 / (obs_error.reshape(-1) * math.sqrt(members - 1)), 0.0)
    anomobs = (picked - pbar) * scale
    innov = (obs_value.reshape(-1) - pbar) * scale
    gram = jnp.dot(anomobs, anomobs.T, precision=precise)
    proj = jnp.dot(anomobs, innov, precision=precise)
    return jnp.concatenate([gram, proj[None]], axis=0)


def domain_reduction(packed):
    packed = lax.psum(packed, ("blk", "sub"))
    return packed


def transform(packed):
    members = packed.shape[1]
    eye = jnp.eye(members, dtype=jnp.float32)
    system = eye + packed[:members]
    proj = packed[members]
    factor_low = jnp.linalg.cholesky(system)
    mean_w = jax.scipy.linalg.cho_solve((factor_low, True), proj)
    scale = jnp.sqrt(jnp.sum(system * system))
    ystate = system / scale
    zstate = eye
    for sweep in range(NS_STEPS):
        factor = 1.5 * eye - 0.5 * jnp.dot(zstate, ystate, precision=precise)
        ystate = jnp.dot(ystate, factor, precision=precise)
        zstate = jnp.dot(factor, zstate, precision=precise)
    return mean_w[:, None] + zstate / jnp.sqrt(scale)


def shards(ensemble, basin_thickness, wet_indicator, obs_cell, obs_count, obs_value, obs_error):
    rows_dev = ensemble.shape[2]
    constant_fields = jnp.stack([basin_thickness, wet_indicator.astype(jnp.float32)])
    total_rows = rows_dev * lax.axis_size("blk")
    rows = (
        lax.axis_index("blk") * rows_dev + jnp.arange(-2, rows_dev + 2, dtype=jnp.int32)
    ).astype(jnp.float32)
    latitude_coupling = (CORIOLIS * (2.0 * (rows + 0.5) / total_rows - 1.0))[:, None]
    dynamic_vector = ensemble
    inner_cor = latitude_coupling[2:-2]
    for number in range(STEPS):
        dynamic_vector = thin_step(dynamic_vector, constant_fields, inner_cor)
    blocks = lax.all_to_all(dynamic_vector, "grid", split_axis=2, concat_axis=0, tiled=True)
    packed = domain_reduction(observe(blocks[:, 0], obs_cell, obs_count, obs_value, obs_error))
    weights = transform(packed)
    members = blocks.shape[0]
    flat = blocks.reshape(members, -1)
    center = jnp.mean(flat, axis=0)
    member_deviations = flat - center
    updated = center + jnp.dot(weights.T, member_deviations, precision=precise)
    return updated.reshape(members, 3, 1, blocks.shape[2], blocks.shape[3])


def solution(mesh):
    placed = (
        P(("copy", "grid"), None, "blk", "sub"),
        P(("copy", "blk"), "sub"),
        P(("copy", "blk"), "sub"),
        P(("copy", "blk"), "grid", "sub", None),
        P(("copy", "blk"), "grid", "sub"),
        P(("copy", "blk"), "grid", "sub", None),
        P(("copy", "blk"), "grid", "sub", None),
    )
    return jax.shard_map(
        shards,
        mesh=mesh,
        in_specs=placed,
        out_specs=P("copy", None, "blk", "grid", "sub"),
        check_vma=False,
    )
```

profile of v0, /device:TPU:0, one launch (start us, length us, event | category | flops | bytes accessed | tf_op | source)
XLA Modules:
  0.0 581.9 jit_solution(4712304430399835638)
XLA Ops:
  0.0 10.2 %fusion.67 = (f32[16,1,128,512]{3,2,1,0:T(8,128)}, f32[16,1,128,512]{3,2,1,0:T(8,128)}, f32[16,1,128,512]{3,2,1,0:T(8,128)S(1)}) fusion(f32[16,3,128,512]{3,2,1,0:T(8,128)} %param.7), kind=kLoop, calls=%fused_computation.164 | loop fusion | bytes 25165824 | tf_op jit(solution)/shard_map/slice | solution.py:42
  10.2 2.4 copy.107
  12.7 2.0 copy-done.5
  14.7 1.3 collective-permute-start
  15.9 4.8 collective-permute-start.1
  20.8 1.5 collective-permute-done.1
  22.4 1.9 pad_maximum_fusion.54
  24.3 0.7 copy.51
  24.9 1.3 collective-permute-start.2
  26.2 0.7 copy.53
  26.9 3.5 collective-permute-start.3
  30.5 0.8 copy.52
  31.3 0.8 copy.54
  32.1 21.8 %multiply_bitcast_fusion.3 = (f32[16,1,128,512]{3,0,2,1:T(8,128)S(1)}, f32[16,128,512]{2,0,1:T(8,128)}, f32[16,1,128,512]{3,0,2,1:T(8,128)}, f32[16,128,512]{2,0,1:T(8,128)}) fusion(f32[128,512]{1,0:T(8,128)S(1)} %copy-done.8, f32[16,128,512]{2,0,1:T(8,128)} %bitcast.143, f32[16,1,512]{2,0,1:T(8,128)S(1)} %collective-permute-done.1, ...), kind=kLoop, calls=%fused_computation.76 | loop fusion | flops 25165824 | bytes 29967104 | tf_op jit(solution)/shard_map/stack | solution.py:50
  53.9 1.0 pad_maximum_fusion.57
  55.0 1.6 collective-permute-start.4
  56.5 4.7 collective-permute-start.5
  61.5 1.6 collective-permute-done.5
  63.1 2.1 pad_maximum_fusion.48
  65.2 2.8 copy.55
  68.1 1.3 collective-permute-start.6
  69.4 1.9 copy.57
  71.2 3.8 collective-permute-start.7
  75.1 2.2 copy.56
  77.3 2.6 copy.58
  79.9 11.1 %bitcast_subtract_fusion = (f32[16,128,512]{2,0,1:T(8,128)S(1)}, f32[16,1,128,512]{3,0,2,1:T(8,128)}) fusion(f32[16,1,128,512]{3,2,1,0:T(8,128)} %copy-done.4, f32[16,2,1,512]{3,0,2,1:T(8,128)S(1)} %collective-permute-done.4, f32[16,1,128,512]{3,0,2,1:T(8,128)} %get-tuple-element.17, f32[16,1,128,512]{3,0,2,1:T(8,128)} %copy-done.2, ...), kind=kLoop, calls=%fused_computation.72 | loop fusion | flops 17825792 | bytes 21135872 | tf_op jit(solution)/shard_map/sub | solution.py:57
  91.0 1.3 collective-permute-start.8
  92.3 4.5 collective-permute-start.9
  96.9 1.6 collective-permute-done.9
  98.9 0.7 copy.59
  99.5 1.3 collective-permute-start.10
  100.8 0.7 copy.61
  101.5 3.0 collective-permute-start.11
  104.5 0.8 copy.60
  105.4 0.8 copy.62
  106.1 17.2 %multiply_bitcast_fusion.1 = (f32[16,1,128,512]{3,0,2,1:T(8,128)S(1)}, f32[16,128,512]{2,0,1:T(8,128)}, f32[16,1,128,512]{3,0,2,1:T(8,128)S(1)}, f32[16,128,512]{2,0,1:T(8,128)}) fusion(f32[128,512]{1,0:T(8,128)} %param.8, f32[16,128,512]{2,0,1:T(8,128)} %copy-done.6, f32[16,1,512]{2,0,1:T(8,128)S(1)} %collective-permute-done.9, ...), kind=kLoop, calls=%fused_computation.74 | loop fusion | flops 25165824 | bytes 29967104 | tf_op jit(solution)/shard_map/stack | solution.py:50
  123.4 1.3 collective-permute-start.12
  124.7 4.5 collective-permute-start.13
  129.6 1.5 collective-permute-done.13
  131.1 2.2 pad_maximum_fusion.44
  133.3 2.8 copy.63
  136.2 1.5 collective-permute-start.14
  137.7 1.3 copy.65
  138.9 3.0 collective-permute-start.15
  142.0 1.5 copy.64
  143.5 2.7 copy.66
  146.1 13.0 %fusion.5 = f32[16,1,128,512]{3,0,2,1:T(8,128)} fusion(f32[16,2,130,1]{3,0,2,1:T(8,128)} %copy.66, f32[16,2,1,512]{3,0,2,1:T(8,128)S(1)} %collective-permute-done.12, f32[16,2,1,512]{3,0,2,1:T(8,128)S(1)} %collective-permute-done.13, f32[16,1,128,512]{3,0,2,1:T(8,128)} %copy-done.1, f32[16,1,128,512]{3,0,2,1:T(8,128)} %copy-done, ...), kind=kLoop, calls=%fused_computation.9 | loop fusion | flops 18874368 | bytes 21135872 | tf_op jit(solution)/shard_map/sub | solution.py:57
  159.1 9.0 %pad_maximum_fusion = f32[16,3,128,512]{3,0,2,1:T(8,128)} fusion(f32[16,1,128,512]{3,0,2,1:T(8,128)} %bitcast.145, f32[16,1,128,512]{3,0,2,1:T(8,128)S(1)} %bitcast.144, f32[16,1,128,512]{3,0,2,1:T(8,128)} %fusion.5), kind=kLoop, calls=%fused_computation.2 | loop fusion | flops 6291456 | bytes 25165824 | tf_op jit(solution)/shard_map/stack | solution.py:58
  168.2 12.1 %copy.67 = f32[16,3,128,512]{3,0,1,2:T(8,128)} copy(f32[16,3,128,512]{3,0,2,1:T(8,128)} %pad_maximum_fusion) | data formatting | bytes 25165824 | tf_op jit(solution)/shard_map/stack | solution.py:58
  180.2 6.8 %all-to-all-start = ((f32[16,3,128,512]{3,0,1,2:T(8,128)}), f32[16,3,128,512]{3,0,1,2:T(8,128)}, u32[]{:S(2)}, u32[]{:S(2)}) async-start(f32[16,3,128,512]{3,0,1,2:T(8,128)} %copy.67), calls=%async_computation | async-start | bytes 25165824 | tf_op jit(solution)/shard_map/all_to_all | solution.py:110
  187.9 273.5 %all-to-all-done = f32[16,3,128,512]{3,0,1,2:T(8,128)} async-done(((f32[16,3,128,512]{3,0,1,2:T(8,128)}), f32[16,3,128,512]{3,0,1,2:T(8,128)}, u32[]{:S(2)}, u32[]{:S(2)}) %all-to-all-start) | async-done | bytes 12582944 | tf_op jit(solution)/shard_map/all_to_all | solution.py:110
  461.4 16.6 %copy.108 = f32[16,3,4,32,512]{4,3,1,0,2:T(8,128)} copy(f32[16,3,4,32,512]{4,0,1,3,2:T(8,128)} %bitcast.10) | data formatting | bytes 25165824 | tf_op jit(solution)/shard_map/all_to_all | solution.py:110
  478.0 5.0 slice.199
  483.0 6.9 %copy.79 = f32[64,1,32,512]{0,3,2,1:T(8,128)} copy(f32[64,1,32,512]{3,2,1,0:T(8,128)} %slice.199) | data formatting | bytes 8388608
  490.0 4.0 gather_fusion
  494.9 11.5 %psum.7 = f32[65,64]{0,1:T(8,128)S(1)} all-reduce(f32[65,64]{0,1:T(8,128)S(1)} %pad_maximum_fusion.59), channel_id=1, replica_groups=mesh['copy'=2,'grid'=4,'blk'=2,'sub'=2] {'blk','sub'}, use_global_device_ids=true, to_apply=%region_2.3 | all-reduce | flops 4160 | bytes 33280 | tf_op jit(solution)/shard_map/psum | solution.py:77
  506.4 0.6 slice_add_fusion
  511.6 11.1 %bitcast_reduce_fusion = f32[3,32,512]{2,1,0:T(8,128)S(1)} fusion(f32[16,3,4,32,512]{4,0,1,3,2:T(8,128)} %bitcast.10), kind=kLoop, calls=%fused_computation.160 | loop fusion | flops 3096576 | bytes 12779520 | tf_op jit(solution)/shard_map/reduce_sum | solution.py:115
  522.8 5.8 %cholesky.26 = f32[64,64]{1,0:T(8,128)S(1)} custom-call(f32[64,64]{1,0:T(8,128)S(1)} %fusion.39), custom_call_target="Cholesky" | custom-call | tf_op jit(solution)/shard_map/jit(cholesky)/cholesky | solution.py:86
  528.9 0.7 compare_reduce_fusion
  530.1 4.9 custom-call.10
  535.4 12.0 %reshape.118 = f32[64,49152]{1,0:T(8,128)} reshape(f32[4,16,3,32,512]{4,3,2,1,0:T(8,128)} %bitcast.139) | data formatting | bytes 25165824 | tf_op jit(solution)/shard_map/reshape | solution.py:114
  547.8 17.4 %convolution_add_fusion = f32[64,49152]{1,0:T(8,128)} fusion(f32[64,64]{1,0:T(8,128)S(1)} %fusion.28, f32[64,49152]{1,0:T(8,128)} %reshape.118, f32[49152]{0:T(1024)S(1)} %bitcast.147), kind=kOutput, calls=%fused_computation.1 | convolution fusion | flops 2422210560 | bytes 25378816 | tf_op jit(solution)/shard_map/dot_general | solution.py:117
  565.2 16.4 %copy.85 = f32[8,8,96,512]{3,2,1,0:T(8,128)} copy(f32[8,8,96,512]{3,1,2,0:T(8,128)} %bitcast.140) | data formatting | bytes 25165824
  (87 shorter events, 7.6 us)
Async XLA Ops:
  10.2 2.4 copy-start.4
  12.6 2.0 copy-start.5
  14.7 6.2 %collective-permute-start = (f32[16,1,512]{2,0,1:T(8,128)S(1)}, f32[16,1,512]{2,0,1:T(8,128)S(1)}, u32[]{:S(2)}, u32[]{:S(2)}) collective-permute-start(f32[16,1,512]{2,0,1:T(8,128)S(1)} %get-tuple-element.39), channel_id=1, source_target_pairs={{2,0},{3,1},{6,4},{7,5},{10,8},{11,9},{14,12},{15,13},{18,16},{19,... | collective-permute-start | bytes 98312 | tf_op jit(solution)/shard_map/ppermute | solution.py:26
  15.9 6.4 %collective-permute-start.1 = (f32[16,1,512]{2,0,1:T(8,128)S(1)}, f32[16,1,512]{2,0,1:T(8,128)S(1)}, u32[]{:S(2)}, u32[]{:S(2)}) collective-permute-start(f32[16,1,512]{2,0,1:T(8,128)S(1)} %get-tuple-element.38), channel_id=1, source_target_pairs={{0,2},{1,3},{4,6},{5,7},{8,10},{9,11},{12,14},{13,15},{16,18},{17,... | collective-permute-start | bytes 98312 | tf_op jit(solution)/shard_map/ppermute | solution.py:24
  20.8 9.6 %copy-start.9 = (s32[128,512]{1,0:T(8,128)S(1)}, s32[128,512]{1,0:T(8,128)}, u32[]{:S(2)}) copy-start(s32[128,512]{1,0:T(8,128)} %param.9) | copy-start | bytes 786436
  20.8 11.3 %copy-start.8 = (f32[128,512]{1,0:T(8,128)S(1)}, f32[128,512]{1,0:T(8,128)}, u32[]{:S(2)}) copy-start(f32[128,512]{1,0:T(8,128)} %param.8) | copy-start | bytes 786436
  24.9 5.6 collective-permute-start.2
  26.9 4.4 collective-permute-start.3
  53.9 9.2 %copy-start.2 = (f32[16,1,128,512]{3,0,2,1:T(8,128)}, f32[16,1,128,512]{3,0,2,1:T(8,128)S(1)}, u32[]{:S(2)}) copy-start(f32[16,1,128,512]{3,0,2,1:T(8,128)S(1)} %get-tuple-element.11) | copy-start | bytes 12582916
  53.9 9.2 %copy-start.3 = (f32[16,1,128,512]{3,0,2,1:T(8,128)S(1)}, f32[16,1,128,512]{3,0,2,1:T(8,128)}, u32[]{:S(2)}) copy-start(f32[16,1,128,512]{3,0,2,1:T(8,128)} %get-tuple-element.17) | copy-start | bytes 12582916
  55.0 6.6 %collective-permute-start.4 = (f32[16,2,1,512]{3,0,2,1:T(8,128)S(1)}, f32[16,2,1,512]{3,0,2,1:T(8,128)S(1)}, u32[]{:S(2)}, u32[]{:S(2)}) collective-permute-start(f32[16,2,1,512]{3,0,2,1:T(8,128)S(1)} %get-tuple-element.31), channel_id=1, source_target_pairs={{2,0},{3,1},{6,4},{7,5},{10,8},{11,9},{14,12},{15,13},{18,16},{19,... | collective-permute-start | bytes 196616 | tf_op jit(solution)/shard_map/ppermute | solution.py:26
  56.5 6.6 %collective-permute-start.5 = (f32[16,2,1,512]{3,0,2,1:T(8,128)S(1)}, f32[16,2,1,512]{3,0,2,1:T(8,128)S(1)}, u32[]{:S(2)}, u32[]{:S(2)}) collective-permute-start(f32[16,2,1,512]{3,0,2,1:T(8,128)S(1)} %get-tuple-element.30), channel_id=1, source_target_pairs={{0,2},{1,3},{4,6},{5,7},{8,10},{9,11},{12,14},{13,15},{16,18},{17,... | collective-permute-start | bytes 196616 | tf_op jit(solution)/shard_map/ppermute | solution.py:24
  68.1 7.0 %collective-permute-start.6 = (f32[16,2,130,1]{2,0,3,1:T(8,128)S(1)}, f32[16,2,130,1]{2,0,3,1:T(8,128)}, u32[]{:S(2)}, u32[]{:S(2)}) collective-permute-start(f32[16,2,130,1]{2,0,3,1:T(8,128)S(1)} %copy.55), channel_id=1, source_target_pairs={{1,0},{3,2},{5,4},{7,6},{9,8},{11,10},{13,12},{15,14},{17,16},{19,... | collective-permute-start | bytes 49928 | tf_op jit(solution)/shard_map/ppermute | solution.py:26
  71.2 6.0 %collective-permute-start.7 = (f32[16,2,130,1]{2,0,3,1:T(8,128)}, f32[16,2,130,1]{2,0,3,1:T(8,128)S(1)}, u32[]{:S(2)}, u32[]{:S(2)}) collective-permute-start(f32[16,2,130,1]{2,0,3,1:T(8,128)} %copy.57), channel_id=1, source_target_pairs={{0,1},{2,3},{4,5},{6,7},{8,9},{10,11},{12,13},{14,15},{16,17},{18,... | collective-permute-start | bytes 49928 | tf_op jit(solution)/shard_map/ppermute | solution.py:24
  91.0 7.5 %copy-start.6 = (f32[16,128,512]{2,0,1:T(8,128)}, f32[16,128,512]{2,0,1:T(8,128)S(1)}, u32[]{:S(2)}) copy-start(f32[16,128,512]{2,0,1:T(8,128)S(1)} %get-tuple-element.9) | copy-start | bytes 12582916
  91.0 5.9 %collective-permute-start.8 = (f32[16,1,512]{2,0,1:T(8,128)S(1)}, f32[16,1,512]{2,0,1:T(8,128)S(1)}, u32[]{:S(2)}, u32[]{:S(2)}) collective-permute-start(f32[16,1,512]{2,0,1:T(8,128)S(1)} %get-tuple-element.37), channel_id=1, source_target_pairs={{2,0},{3,1},{6,4},{7,5},{10,8},{11,9},{14,12},{15,13},{18,16},{19,... | collective-permute-start | bytes 98312 | tf_op jit(solution)/shard_map/ppermute | solution.py:26
  92.3 6.1 %collective-permute-start.9 = (f32[16,1,512]{2,0,1:T(8,128)S(1)}, f32[16,1,512]{2,0,1:T(8,128)S(1)}, u32[]{:S(2)}, u32[]{:S(2)}) collective-permute-start(f32[16,1,512]{2,0,1:T(8,128)S(1)} %get-tuple-element.36), channel_id=1, source_target_pairs={{0,2},{1,3},{4,6},{5,7},{8,10},{9,11},{12,14},{13,15},{16,18},{17,... | collective-permute-start | bytes 98312 | tf_op jit(solution)/shard_map/ppermute | solution.py:24
  99.5 5.0 collective-permute-start.10
  101.5 3.9 collective-permute-start.11
  123.3 7.8 %copy-start = (f32[16,1,128,512]{3,0,2,1:T(8,128)}, f32[16,1,128,512]{3,0,2,1:T(8,128)S(1)}, u32[]{:S(2)}) copy-start(f32[16,1,128,512]{3,0,2,1:T(8,128)S(1)} %get-tuple-element.5) | copy-start | bytes 12582916
  123.3 7.8 %copy-start.1 = (f32[16,1,128,512]{3,0,2,1:T(8,128)}, f32[16,1,128,512]{3,0,2,1:T(8,128)S(1)}, u32[]{:S(2)}) copy-start(f32[16,1,128,512]{3,0,2,1:T(8,128)S(1)} %get-tuple-element.15) | copy-start | bytes 12582916
  123.4 6.2 %collective-permute-start.12 = (f32[16,2,1,512]{3,0,2,1:T(8,128)S(1)}, f32[16,2,1,512]{3,0,2,1:T(8,128)S(1)}, u32[]{:S(2)}, u32[]{:S(2)}) collective-permute-start(f32[16,2,1,512]{3,0,2,1:T(8,128)S(1)} %get-tuple-element.29), channel_id=1, source_target_pairs={{2,0},{3,1},{6,4},{7,5},{10,8},{11,9},{14,12},{15,13},{18,16},{19,... | collective-permute-start | bytes 196616 | tf_op jit(solution)/shard_map/ppermute | solution.py:26
  124.7 6.4 %collective-permute-start.13 = (f32[16,2,1,512]{3,0,2,1:T(8,128)S(1)}, f32[16,2,1,512]{3,0,2,1:T(8,128)S(1)}, u32[]{:S(2)}, u32[]{:S(2)}) collective-permute-start(f32[16,2,1,512]{3,0,2,1:T(8,128)S(1)} %get-tuple-element.28), channel_id=1, source_target_pairs={{0,2},{1,3},{4,6},{5,7},{8,10},{9,11},{12,14},{13,15},{16,18},{17,... | collective-permute-start | bytes 196616 | tf_op jit(solution)/shard_map/ppermute | solution.py:24
  136.2 5.8 collective-permute-start.14
  138.9 4.5 collective-permute-start.15
  146.1 13.0 %copy-start.7 = (f32[16,128,512]{2,0,1:T(8,128)S(1)}, f32[16,128,512]{2,0,1:T(8,128)}, u32[]{:S(2)}) copy-start(f32[16,128,512]{2,0,1:T(8,128)} %get-tuple-element.6) | copy-start | bytes 12582916
  180.2 7.6 %copy-start.11 = (s32[1,1,1,64]{3,2,1,0:T(1,128)S(1)}, s32[1,1,1,64]{3,2,1,0:T(1,128)}, u32[]{:S(2)}) copy-start(s32[1,1,1,64]{3,2,1,0:T(1,128)} %param.10) | copy-start | bytes 772
  180.2 281.1 %all-to-all-start = ((f32[16,3,128,512]{3,0,1,2:T(8,128)}), f32[16,3,128,512]{3,0,1,2:T(8,128)}, u32[]{:S(2)}, u32[]{:S(2)}) async-start(f32[16,3,128,512]{3,0,1,2:T(8,128)} %copy.67), calls=%async_computation | async-start | bytes 25165824 | tf_op jit(solution)/shard_map/all_to_all | solution.py:110
  483.0 11.1 %copy-start.10 = (f32[1,1,1,64]{3,2,1,0:T(1,128)S(1)}, f32[1,1,1,64]{3,2,1,0:T(1,128)}, u32[]{:S(2)}) copy-start(f32[1,1,1,64]{3,2,1,0:T(1,128)} %param.13) | copy-start | bytes 772
  483.0 11.4 %copy-start.12 = (f32[1,1,1,64]{3,2,1,0:T(1,128)S(1)}, f32[1,1,1,64]{3,2,1,0:T(1,128)}, u32[]{:S(2)}) copy-start(f32[1,1,1,64]{3,2,1,0:T(1,128)} %param.12) | copy-start | bytes 772
where the time goes:
time: 588 us; the launch traced here: 582 us
  waiting for transfers between devices  280 us (48%)
  local copies, waits for them, and re-layouts  112 us (19%)
  other arithmetic  104 us (18%)
  starting transfers between devices  49.6 us (8%)
  matrix products  22.2 us (4%)
  blocking collectives  11.5 us (2%)
    all_to_all x1, waiting for transfers between devices, shards(): lax.all_to_all(dynamic_vector, 'grid', split_axis=2, concat_axis=0, tiled...  273 us
    another operation x4, other arithmetic, thin_step(): jnp.stack([inner_depth * first_new, inner_depth * second_new], axis=1)  40 us
    ppermute x8, starting transfers between devices, padded(): lax.ppermute(tail, axis, [(i, (i + 1) % count) for i in range(ends)])  32 us
    unnamed x30, local copies, waits for them, and re-layouts  27.9 us
    sub x2, other arithmetic, thin_step(): height_new = height - DIVERGE * divergence  24.1 us
    dot_general x1, matrix products, shards(): updated = center + jnp.dot(weights.T, member_deviations, precision=precise)  17.4 us
    all_to_all x1, local copies, waits for them, and re-layouts, shards(): lax.all_to_all(dynamic_vector, 'grid', split_axis=2, concat_axis=0, tiled...  16.6 us
    another operation x1, local copies, waits for them, and re-layouts, thin_step(): return jnp.stack([height_new, first_new, second_new], axis=1)  12.1 us
  transfers between devices with their start and end apart: 17, of which 7 were waited for; matrix products, arithmetic and copies ran while one was open for 2% of the time, Pallas kernels for 0%

commit v1 on v0

--- a/solution.py
+++ b/solution.py
@@ -107,7 +107,12 @@
     inner_cor = latitude_coupling[2:-2]
     for number in range(STEPS):
         dynamic_vector = thin_step(dynamic_vector, constant_fields, inner_cor)
-    blocks = lax.all_to_all(dynamic_vector, "grid", split_axis=2, concat_axis=0, tiled=True)
+    blocks = jnp.concatenate(
+        lax.all_to_all(
+            jnp.stack(jnp.split(dynamic_vector, lax.axis_size("grid"), axis=2)), "grid", 0, 0
+        ),
+        axis=0,
+    )
     packed = domain_reduction(observe(blocks[:, 0], obs_cell, obs_count, obs_value, obs_error))
     weights = transform(packed)
     members = blocks.shape[0]

time: 588 us -> 564 us (0.959)
  local copies, waits for them, and re-layouts: 112 us -> 87.9 us
    all_to_all x1 -> x0, local copies, waits for them, and re-layouts: 16.6 us -> none  [shards(): lax.all_to_all(dynamic_vector, 'grid', split_axis=2, concat_axis=0, tiled...]
    reshape x1 -> x0, local copies, waits for them, and re-layouts: 12 us -> none  [shards(): flat = blocks.reshape(members, -1)]
    another operation x4, other arithmetic: 40 us -> 29.5 us  [thin_step(): jnp.stack([inner_depth * first_new, inner_depth * second_new], axis=1)]
    slice x1 -> x0, local copies, waits for them, and re-layouts: 10.2 us -> none  [thin_step(): dynamic_vector[:, 2]]
    another operation x1 -> x2, local copies, waits for them, and re-layouts: 12.1 us -> 21.5 us  [the longest x1 12 us: shards(): flat = blocks.reshape(members, -1)]
    unnamed x30 -> x24, local copies, waits for them, and re-layouts: 27.9 us -> 18.5 us
    another operation x0 -> x1, other arithmetic: none -> 7.9 us  [shards(): jnp.stack(jnp.split(dynamic_vector, lax.axis_size('grid'), axis=2))]
    slice x1 -> x2, local copies, waits for them, and re-layouts: 5 us -> 11.9 us  [shards(): blocks[:, 0]]
  transfers between devices with their start and end apart: 17 -> 17, of which waited for: 7 -> 9; matrix products, arithmetic and copies ran while one was open for 2% -> 2% of each run, Pallas kernels for 0% -> 0%
where the time goes in v1:
time: 564 us; the launch traced here: 554 us
  waiting for transfers between devices  281 us (50%)
  other arithmetic  103 us (18%)
  local copies, waits for them, and re-layouts  87.9 us (16%)
  starting transfers between devices  47.4 us (8%)
  matrix products  21.8 us (4%)
  blocking collectives  11.4 us (2%)
    all_to_all x1, waiting for transfers between devices, shards(): lax.all_to_all(jnp.stack(jnp.split(dynamic_vector, lax.axis_size('grid'),...  273 us
    ppermute x8, starting transfers between devices, padded(): lax.ppermute(tail, axis, [(i, (i + 1) % count) for i in range(ends)])  30.6 us
    another operation x4, other arithmetic, thin_step(): jnp.stack([inner_depth * first_new, inner_depth * second_new], axis=1)  29.5 us
    sub x2, other arithmetic, thin_step(): height_new = height - DIVERGE * divergence  25.9 us
    unnamed x24, local copies, waits for them, and re-layouts  18.5 us
    dot_general x1, matrix products, shards(): updated = center + jnp.dot(weights.T, member_deviations, precision=precise)  17 us
    another operation x1, local copies, waits for them, and re-layouts, shards(): flat = blocks.reshape(members, -1)  12 us
    slice x2, local copies, waits for them, and re-layouts, shards(): blocks[:, 0]  11.9 us
  transfers between devices with their start and end apart: 17, of which 9 were waited for; matrix products, arithmetic and copies ran while one was open for 2% of the time, Pallas kernels for 0%

profile of v1, /device:TPU:0, one launch (start us, length us, event | category | flops | bytes accessed | tf_op | source)
XLA Modules:
  0.0 554.4 jit_solution(11699586528180589546)
XLA Ops:
  0.0 2.9 slice_bitcast_fusion
  2.9 2.0 copy-done.5
  5.0 1.3 collective-permute-start
  6.3 4.8 collective-permute-start.1
  11.1 1.6 collective-permute-done.1
  12.7 2.0 pad_maximum_fusion.55
  14.7 0.6 copy.47
  15.3 1.3 collective-permute-start.2
  16.6 0.6 copy.49
  17.2 3.0 collective-permute-start.3
  20.4 0.4 copy.48
  21.1 1.5 copy.50
  22.5 14.6 %multiply_bitcast_fusion.3 = (f32[16,1,128,512]{3,2,0,1:T(8,128)S(1)}, f32[16,128,512]{2,1,0:T(8,128)}, f32[16,1,128,512]{3,2,0,1:T(8,128)S(1)}, f32[16,128,512]{2,1,0:T(8,128)}) fusion(f32[128,512]{1,0:T(8,128)} %param.8, f32[16,128,512]{2,1,0:T(8,128)} %copy-done.5, f32[16,1,512]{2,1,0:T(1,128)S(1)} %collective-permute-done.1, ...), kind=kLoop, calls=%fused_computation.83 | loop fusion | flops 25165824 | bytes 29967104 | tf_op jit(solution)/shard_map/stack | solution.py:50
  37.3 1.3 collective-permute-start.4
  38.6 4.5 collective-permute-start.5
  43.5 1.5 collective-permute-done.5
  45.1 3.0 pad_maximum_fusion.49
  48.0 2.8 copy.51
  50.9 1.3 collective-permute-start.6
  52.2 2.8 copy.53
  55.0 3.0 collective-permute-start.7
  58.0 2.1 copy.52
  60.1 2.1 copy.54
  62.3 12.8 %bitcast_subtract_fusion.1 = (f32[16,128,512]{2,1,0:T(8,128)S(1)}, f32[16,1,128,512]{3,2,0,1:T(8,128)}) fusion(f32[16,3,128,512]{3,2,1,0:T(8,128)} %param.7, f32[16,2,1,512]{3,2,0,1:T(1,128)S(1)} %collective-permute-done.4, f32[16,1,128,512]{3,2,0,1:T(8,128)} %copy-done.3, f32[16,1,128,512]{3,2,0,1:T(8,128)} %copy-done.2, ...), kind=kLoop, calls=%fused_computation.79 | loop fusion | flops 17825792 | bytes 21135872 | tf_op jit(solution)/shard_map/sub | solution.py:57
  75.2 1.3 collective-permute-start.8
  76.5 4.5 collective-permute-start.9
  81.0 1.6 collective-permute-done.9
  82.6 1.9 pad_maximum_fusion.52
  84.5 1.8 copy.55
  86.3 1.3 collective-permute-start.10
  87.6 1.9 copy.57
  89.5 3.0 collective-permute-start.11
  92.5 0.4 copy.56
  93.3 1.5 copy.58
  94.8 14.7 %multiply_bitcast_fusion.1 = (f32[16,1,128,512]{3,2,0,1:T(8,128)S(1)}, f32[16,128,512]{2,1,0:T(8,128)}, f32[16,1,128,512]{3,2,0,1:T(8,128)S(1)}, f32[16,128,512]{2,1,0:T(8,128)}) fusion(f32[128,512]{1,0:T(8,128)} %param.8, f32[16,128,512]{2,1,0:T(8,128)} %copy-done.4, f32[16,1,512]{2,1,0:T(1,128)S(1)} %collective-permute-done.9, ...), kind=kLoop, calls=%fused_computation.81 | loop fusion | flops 25165824 | bytes 29967104 | tf_op jit(solution)/shard_map/stack | solution.py:50
  109.6 1.3 collective-permute-start.12
  110.9 4.5 collective-permute-start.13
  115.8 1.5 collective-permute-done.13
  117.3 3.1 pad_maximum_fusion.45
  120.4 2.8 copy.59
  123.2 1.3 collective-permute-start.14
  124.5 2.8 copy.61
  127.3 3.0 collective-permute-start.15
  130.4 2.2 copy.60
  132.6 2.1 copy.62
  134.7 13.0 %fusion.6 = f32[16,1,128,512]{3,2,1,0:T(8,128)} fusion(f32[16,2,130,1]{3,2,0,1:T(8,128)} %copy.62, f32[16,2,1,512]{3,2,0,1:T(1,128)S(1)} %collective-permute-done.12, f32[16,2,1,512]{3,2,0,1:T(1,128)S(1)} %collective-permute-done.13, f32[16,1,128,512]{3,2,0,1:T(8,128)} %copy-done.1, f32[16,1,128,512]{3,2,0,1:T(8,128)} %copy-done, ...), kind=kLoop, calls=%fused_computation.11 | loop fusion | flops 18874368 | bytes 21135872 | tf_op jit(solution)/shard_map/sub | solution.py:57
  147.7 10.6 %pad_maximum_fusion = f32[16,3,128,512]{3,2,1,0:T(8,128)} fusion(f32[16,1,128,512]{3,2,1,0:T(8,128)} %bitcast.160, f32[16,1,128,512]{3,2,1,0:T(8,128)S(1)} %bitcast.159, f32[16,1,128,512]{3,2,1,0:T(8,128)} %fusion.6), kind=kLoop, calls=%fused_computation.2 | loop fusion | flops 6291456 | bytes 25165824 | tf_op jit(solution)/shard_map/stack | solution.py:58
  158.3 9.5 %slice_bitcast_fusion.4 = (f32[1,16,3,32,512]{4,3,2,1,0:T(8,128)S(1)}, f32[1,16,3,32,512]{4,3,2,1,0:T(8,128)S(1)}, f32[1,16,3,32,512]{4,3,2,1,0:T(8,128)}, f32[1,16,3,32,512]{4,3,2,1,0:T(8,128)}) fusion(f32[16,3,128,512]{3,2,1,0:T(8,128)} %pad_maximum_fusion), kind=kLoop, calls=%fused_computation.88 | loop fusion | bytes 25165824 | tf_op jit(solution)/shard_map/stack | solution.py:112
  167.8 7.9 %pad_maximum_fusion.1 = f32[4,16,3,32,512]{4,3,2,1,0:T(8,128)} fusion(f32[1,16,3,32,512]{4,3,2,1,0:T(8,128)S(1)} %get-tuple-element.20, f32[1,16,3,32,512]{4,3,2,1,0:T(8,128)} %get-tuple-element.21, f32[1,16,3,32,512]{4,3,2,1,0:T(8,128)} %get-tuple-element.22, f32[1,16,3,32,512]{4,3,2,1,0:T(8,128)S(1)} %get-tuple-element.19), kind=kLoop, calls=%fused_computation.3 | loop fusion | flops 9437184 | bytes 25165824 | tf_op jit(solution)/shard_map/stack | solution.py:112
  175.7 6.4 %all-to-all-start = ((f32[4,16,3,32,512]{4,3,2,1,0:T(8,128)}), f32[4,16,3,32,512]{4,3,2,1,0:T(8,128)}, u32[]{:S(2)}, u32[]{:S(2)}) async-start(f32[4,16,3,32,512]{4,3,2,1,0:T(8,128)} %pad_maximum_fusion.1), calls=%async_computation | async-start | bytes 25165824 | tf_op jit(solution)/shard_map/all_to_all | solution.py:111
  183.0 273.2 %all-to-all-done = f32[4,16,3,32,512]{4,3,2,1,0:T(8,128)} async-done(((f32[4,16,3,32,512]{4,3,2,1,0:T(8,128)}), f32[4,16,3,32,512]{4,3,2,1,0:T(8,128)}, u32[]{:S(2)}, u32[]{:S(2)}) %all-to-all-start) | async-done | bytes 12582944 | tf_op jit(solution)/shard_map/all_to_all | solution.py:111
  456.1 4.9 slice.199
  461.1 6.9 %copy.65 = f32[64,1,32,512]{0,3,2,1:T(8,128)} copy(f32[64,1,32,512]{3,2,1,0:T(8,128)} %slice.199) | data formatting | bytes 8388608 | tf_op jit(solution)/shard_map/slice | solution.py:116
  468.0 4.0 gather_fusion
  473.0 11.4 %psum.7 = f32[65,64]{0,1:T(8,128)S(1)} all-reduce(f32[65,64]{0,1:T(8,128)S(1)} %pad_maximum_fusion.60), channel_id=1, replica_groups=mesh['copy'=2,'grid'=4,'blk'=2,'sub'=2] {'blk','sub'}, use_global_device_ids=true, to_apply=%region_2.3 | all-reduce | flops 4160 | bytes 33280 | tf_op jit(solution)/shard_map/psum | solution.py:77
  484.4 0.6 slice_add_fusion
  489.7 5.8 %cholesky.26 = f32[64,64]{1,0:T(8,128)S(1)} custom-call(f32[64,64]{1,0:T(8,128)S(1)} %fusion.42), custom_call_target="Cholesky" | custom-call | tf_op jit(solution)/shard_map/jit(cholesky)/cholesky | solution.py:86
  495.8 0.6 compare_reduce_fusion
  496.4 0.7 fusion.39
  497.1 4.9 custom-call.10
  502.3 5.8 %reduce_sum.27 = f32[3,32,512]{2,1,0:T(8,128)S(1)} reduce(f32[4,16,3,32,512]{4,3,2,1,0:T(8,128)} %all-to-all-done, f32[]{:T(128)} %constant.91.clone.1), dimensions={0,1}, to_apply=%region_0.1 | reduce | flops 3096576 | bytes 12779524 | tf_op jit(solution)/shard_map/reduce_sum | solution.py:120
  508.5 12.0 %reshape_reshape.3 = f32[64,49152]{1,0:T(8,128)} reshape(f32[4,16,3,32,512]{4,3,2,1,0:T(8,128)} %all-to-all-done) | data formatting | bytes 25165824 | tf_op jit(solution)/shard_map/reshape;reshape | solution.py:119
  520.5 17.0 %convolution_add_fusion = f32[64,49152]{1,0:T(8,128)} fusion(f32[64,64]{1,0:T(8,128)S(1)} %fusion.31, f32[64,49152]{1,0:T(8,128)} %reshape_reshape.3, f32[49152]{0:T(1024)S(1)} %bitcast.162), kind=kOutput, calls=%fused_computation.1 | convolution fusion | flops 2422210560 | bytes 25378816 | tf_op jit(solution)/shard_map/dot_general | solution.py:122
  537.6 16.4 %copy.80 = f32[8,8,96,512]{3,2,1,0:T(8,128)} copy(f32[8,8,96,512]{3,1,2,0:T(8,128)} %bitcast.158) | data formatting | bytes 25165824
  (82 shorter events, 7.6 us)
Async XLA Ops:
  2.9 2.0 copy-start.5
  5.0 6.2 %collective-permute-start = (f32[16,1,512]{2,1,0:T(1,128)S(1)}, f32[16,1,512]{2,1,0:T(1,128)S(1)}, u32[]{:S(2)}, u32[]{:S(2)}) collective-permute-start(f32[16,1,512]{2,1,0:T(1,128)S(1)} %get-tuple-element.38), channel_id=1, source_target_pairs={{2,0},{3,1},{6,4},{7,5},{10,8},{11,9},{14,12},{15,13},{18,16},{19,... | collective-permute-start | bytes 98312 | tf_op jit(solution)/shard_map/ppermute | solution.py:26
  6.3 6.4 %collective-permute-start.1 = (f32[16,1,512]{2,1,0:T(1,128)S(1)}, f32[16,1,512]{2,1,0:T(1,128)S(1)}, u32[]{:S(2)}, u32[]{:S(2)}) collective-permute-start(f32[16,1,512]{2,1,0:T(1,128)S(1)} %get-tuple-element.37), channel_id=1, source_target_pairs={{0,2},{1,3},{4,6},{5,7},{8,10},{9,11},{12,14},{13,15},{16,18},{17,... | collective-permute-start | bytes 98312 | tf_op jit(solution)/shard_map/ppermute | solution.py:24
  11.1 9.1 %copy-start.7 = (s32[128,512]{1,0:T(8,128)S(1)}, s32[128,512]{1,0:T(8,128)}, u32[]{:S(2)}) copy-start(s32[128,512]{1,0:T(8,128)} %param.9) | copy-start | bytes 786436
  15.3 5.1 collective-permute-start.2
  17.2 3.9 collective-permute-start.3
  37.2 7.9 %copy-start.2 = (f32[16,1,128,512]{3,2,0,1:T(8,128)}, f32[16,1,128,512]{3,2,0,1:T(8,128)S(1)}, u32[]{:S(2)}) copy-start(f32[16,1,128,512]{3,2,0,1:T(8,128)S(1)} %get-tuple-element.11) | copy-start | bytes 12582916
  37.2 7.9 %copy-start.3 = (f32[16,1,128,512]{3,2,0,1:T(8,128)}, f32[16,1,128,512]{3,2,0,1:T(8,128)S(1)}, u32[]{:S(2)}) copy-start(f32[16,1,128,512]{3,2,0,1:T(8,128)S(1)} %get-tuple-element.15) | copy-start | bytes 12582916
  37.3 6.2 %collective-permute-start.4 = (f32[16,2,1,512]{3,2,0,1:T(1,128)S(1)}, f32[16,2,1,512]{3,2,0,1:T(1,128)S(1)}, u32[]{:S(2)}, u32[]{:S(2)}) collective-permute-start(f32[16,2,1,512]{3,2,0,1:T(1,128)S(1)} %get-tuple-element.30), channel_id=1, source_target_pairs={{2,0},{3,1},{6,4},{7,5},{10,8},{11,9},{14,12},{15,13},{18,16},{19,... | collective-permute-start | bytes 196616 | tf_op jit(solution)/shard_map/ppermute | solution.py:26
  38.6 6.4 %collective-permute-start.5 = (f32[16,2,1,512]{3,2,0,1:T(1,128)S(1)}, f32[16,2,1,512]{3,2,0,1:T(1,128)S(1)}, u32[]{:S(2)}, u32[]{:S(2)}) collective-permute-start(f32[16,2,1,512]{3,2,0,1:T(1,128)S(1)} %get-tuple-element.29), channel_id=1, source_target_pairs={{0,2},{1,3},{4,6},{5,7},{8,10},{9,11},{12,14},{13,15},{16,18},{17,... | collective-permute-start | bytes 196616 | tf_op jit(solution)/shard_map/ppermute | solution.py:24
  50.9 7.2 %collective-permute-start.6 = (f32[16,2,130,1]{2,0,3,1:T(8,128)S(1)}, f32[16,2,130,1]{2,0,3,1:T(8,128)S(1)}, u32[]{:S(2)}, u32[]{:S(2)}) collective-permute-start(f32[16,2,130,1]{2,0,3,1:T(8,128)S(1)} %copy.51), channel_id=1, source_target_pairs={{1,0},{3,2},{5,4},{7,6},{9,8},{11,10},{13,12},{15,14},{17,16},{19,... | collective-permute-start | bytes 49928 | tf_op jit(solution)/shard_map/ppermute | solution.py:26
  55.0 5.2 collective-permute-start.7
  75.1 7.5 %copy-start.4 = (f32[16,128,512]{2,1,0:T(8,128)}, f32[16,128,512]{2,1,0:T(8,128)S(1)}, u32[]{:S(2)}) copy-start(f32[16,128,512]{2,1,0:T(8,128)S(1)} %get-tuple-element.9) | copy-start | bytes 12582916
  75.2 5.9 %collective-permute-start.8 = (f32[16,1,512]{2,1,0:T(1,128)S(1)}, f32[16,1,512]{2,1,0:T(1,128)S(1)}, u32[]{:S(2)}, u32[]{:S(2)}) collective-permute-start(f32[16,1,512]{2,1,0:T(1,128)S(1)} %get-tuple-element.36), channel_id=1, source_target_pairs={{2,0},{3,1},{6,4},{7,5},{10,8},{11,9},{14,12},{15,13},{18,16},{19,... | collective-permute-start | bytes 98312 | tf_op jit(solution)/shard_map/ppermute | solution.py:26
  76.5 6.1 %collective-permute-start.9 = (f32[16,1,512]{2,1,0:T(1,128)S(1)}, f32[16,1,512]{2,1,0:T(1,128)S(1)}, u32[]{:S(2)}, u32[]{:S(2)}) collective-permute-start(f32[16,1,512]{2,1,0:T(1,128)S(1)} %get-tuple-element.35), channel_id=1, source_target_pairs={{0,2},{1,3},{4,6},{5,7},{8,10},{9,11},{12,14},{13,15},{16,18},{17,... | collective-permute-start | bytes 98312 | tf_op jit(solution)/shard_map/ppermute | solution.py:24
  86.3 6.2 %collective-permute-start.10 = (f32[16,130,1]{1,0,2:T(8,128)S(1)}, f32[16,130,1]{1,0,2:T(8,128)S(1)}, u32[]{:S(2)}, u32[]{:S(2)}) collective-permute-start(f32[16,130,1]{1,0,2:T(8,128)S(1)} %copy.55), channel_id=1, source_target_pairs={{1,0},{3,2},{5,4},{7,6},{9,8},{11,10},{13,12},{15,14},{17,16},{19,... | collective-permute-start | bytes 24968 | tf_op jit(solution)/shard_map/ppermute | solution.py:26
  89.5 3.9 collective-permute-start.11
  109.4 7.9 %copy-start = (f32[16,1,128,512]{3,2,0,1:T(8,128)}, f32[16,1,128,512]{3,2,0,1:T(8,128)S(1)}, u32[]{:S(2)}) copy-start(f32[16,1,128,512]{3,2,0,1:T(8,128)S(1)} %get-tuple-element.5) | copy-start | bytes 12582916
  109.5 7.9 %copy-start.1 = (f32[16,1,128,512]{3,2,0,1:T(8,128)}, f32[16,1,128,512]{3,2,0,1:T(8,128)S(1)}, u32[]{:S(2)}) copy-start(f32[16,1,128,512]{3,2,0,1:T(8,128)S(1)} %get-tuple-element.17) | copy-start | bytes 12582916
  109.6 6.2 %collective-permute-start.12 = (f32[16,2,1,512]{3,2,0,1:T(1,128)S(1)}, f32[16,2,1,512]{3,2,0,1:T(1,128)S(1)}, u32[]{:S(2)}, u32[]{:S(2)}) collective-permute-start(f32[16,2,1,512]{3,2,0,1:T(1,128)S(1)} %get-tuple-element.28), channel_id=1, source_target_pairs={{2,0},{3,1},{6,4},{7,5},{10,8},{11,9},{14,12},{15,13},{18,16},{19,... | collective-permute-start | bytes 196616 | tf_op jit(solution)/shard_map/ppermute | solution.py:26
  110.9 6.4 %collective-permute-start.13 = (f32[16,2,1,512]{3,2,0,1:T(1,128)S(1)}, f32[16,2,1,512]{3,2,0,1:T(1,128)S(1)}, u32[]{:S(2)}, u32[]{:S(2)}) collective-permute-start(f32[16,2,1,512]{3,2,0,1:T(1,128)S(1)} %get-tuple-element.27), channel_id=1, source_target_pairs={{0,2},{1,3},{4,6},{5,7},{8,10},{9,11},{12,14},{13,15},{16,18},{17,... | collective-permute-start | bytes 196616 | tf_op jit(solution)/shard_map/ppermute | solution.py:24
  123.2 7.2 %collective-permute-start.14 = (f32[16,2,130,1]{2,0,3,1:T(8,128)S(1)}, f32[16,2,130,1]{2,0,3,1:T(8,128)S(1)}, u32[]{:S(2)}, u32[]{:S(2)}) collective-permute-start(f32[16,2,130,1]{2,0,3,1:T(8,128)S(1)} %copy.59), channel_id=1, source_target_pairs={{1,0},{3,2},{5,4},{7,6},{9,8},{11,10},{13,12},{15,14},{17,16},{19,... | collective-permute-start | bytes 49928 | tf_op jit(solution)/shard_map/ppermute | solution.py:26
  127.3 5.2 collective-permute-start.15
  134.7 13.0 %copy-start.6 = (f32[16,128,512]{2,1,0:T(8,128)S(1)}, f32[16,128,512]{2,1,0:T(8,128)}, u32[]{:S(2)}) copy-start(f32[16,128,512]{2,1,0:T(8,128)} %get-tuple-element.6) | copy-start | bytes 12582916
  175.7 7.2 %copy-start.9 = (s32[1,1,1,64]{3,2,1,0:T(1,128)S(1)}, s32[1,1,1,64]{3,2,1,0:T(1,128)}, u32[]{:S(2)}) copy-start(s32[1,1,1,64]{3,2,1,0:T(1,128)} %param.10) | copy-start | bytes 772
  175.7 280.4 %all-to-all-start = ((f32[4,16,3,32,512]{4,3,2,1,0:T(8,128)}), f32[4,16,3,32,512]{4,3,2,1,0:T(8,128)}, u32[]{:S(2)}, u32[]{:S(2)}) async-start(f32[4,16,3,32,512]{4,3,2,1,0:T(8,128)} %pad_maximum_fusion.1), calls=%async_computation | async-start | bytes 25165824 | tf_op jit(solution)/shard_map/all_to_all | solution.py:111
  461.1 11.1 %copy-start.8 = (f32[1,1,1,64]{3,2,1,0:T(1,128)S(1)}, f32[1,1,1,64]{3,2,1,0:T(1,128)}, u32[]{:S(2)}) copy-start(f32[1,1,1,64]{3,2,1,0:T(1,128)} %param.13) | copy-start | bytes 772
  461.1 11.5 %copy-start.10 = (f32[1,1,1,64]{3,2,1,0:T(1,128)S(1)}, f32[1,1,1,64]{3,2,1,0:T(1,128)}, u32[]{:S(2)}) copy-start(f32[1,1,1,64]{3,2,1,0:T(1,128)} %param.12) | copy-start | bytes 772
